TPU v7x, 32 devices: a whole 2x2x4 slice. The times are simulated.
32 devices in a mesh: parts: 1, head: 32 (over z, y, x, core).
Axes of the slice: x: 2, y: 2, z: 4, core: 2. Of those that a mesh axis runs over, the one named last changes fastest.
Arguments:
- queries: bfloat16 [8, 2048, 2048], P('parts', 'head'), may hold values from -6 to 6
- keys: bfloat16 [8, 2048, 2048], P('parts', 'head'), may hold values from -6 to 6
- values: bfloat16 [8, 2048, 2048], P('parts', 'head'), may hold values from -6 to 6
- slot_positions: int32 [8, 2048], P('parts', 'head'), may hold values from 0 to 2047, each once within a row
- counts: int32 [8], P('parts'), may hold values from 16 to 2048, as said below
- timesteps: int32 [8], P('parts'), may hold values from 0 to 999
- labels: int32 [8], P('parts'), may hold values from 0 to 127
- time_weight: bfloat16 [256, 4096], replicated, may hold values from -0.375 to 0.375
- norm_gain: float32 [2048], replicated, may hold values from 0.25 to 1.75
- gate_weight: bfloat16 [2048, 8192], P(None, 'head'), may hold values from -0.125 to 0.125
- up_weight: bfloat16 [2048, 8192], P(None, 'head'), may hold values from -0.125 to 0.125
- down_weight: bfloat16 [8192, 2048], P('head'), may hold values from -0.0625 to 0.0625
- class_weight: bfloat16 [2048, 128], replicated, may hold values from -3 to 3
- class_bias: float32 [128], replicated, may hold values from -5 to 112
Outputs:
- attention: bfloat16 [256, 2048, 64], P(('parts', 'head'))
- guidance: float32 [8, 128, 2048], P('parts', 'head')
Inputs may be any that keep to these rules, and one draw needn't show every extreme that they name: `counts`: multiples of 16; in every part one shower has exactly 2048. `slot_positions`: each shower's row is a permutation of 0 to 2047.
All inputs are finite; a program needn't handle non-finite values.
Results may differ from a plain program's by a relative error of at most 0.01.
The roundings to bfloat16 on the way count: a program that leaves them out, or rounds other values in their place, can miss the bound.
Values may be sent and summed in bfloat16 or wider, within the bound.
A program may use at most 192 MiB of HBM per device.

v0:
```python
import math

import jax
import jax.numpy as jnp
from jax import lax
from jax.sharding import PartitionSpec as P

HEADS = 32
POOL = 16


epsilon = 1e-06


def sinusoid(steps, embed_width):
    half_width = embed_width // 2
    frequency = jnp.exp(-math.log(10000.0) * jnp.arange(half_width, dtype=jnp.float32) / half_width)
    angles = steps.astype(jnp.float32)[:, None] * frequency[None, :]
    return jnp.concatenate([jnp.cos(angles), jnp.sin(angles)], axis=1)


def attend_pair(pair_data):
    query_rows, key_rows, value_rows, key_valid = pair_data
    head_dim = query_rows.shape[1]
    scores = jnp.dot(query_rows, key_rows.T, preferred_element_type=jnp.float32) * head_dim ** (
        -0.5
    )
    scores = jnp.where(key_valid[None, :], scores, -jnp.inf)
    peak = jnp.max(scores, axis=1, keepdims=True)
    exponent = jnp.exp(scores - peak)
    weights = (exponent / jnp.sum(exponent, axis=1, keepdims=True)).astype(jnp.bfloat16)
    mixed = jnp.dot(weights, value_rows, preferred_element_type=jnp.float32)
    return (mixed * key_valid[:, None].astype(jnp.float32)).astype(jnp.bfloat16)


def body(
    queries,
    keys,
    values,
    slot_positions,
    counts,
    timesteps,
    labels,
    time_weight,
    norm_gain,
    gate_weight,
    up_weight,
    down_weight,
    class_weight,
    class_bias,
):
    devices = lax.axis_size("head")
    device_index = lax.axis_index("head")
    showers, local_length, model_width = queries.shape
    head_dim = model_width // HEADS
    pairs_here = showers * HEADS // devices
    windows = local_length * devices // POOL
    per_device = windows // devices
    row_total = showers * windows

    def to_pairs(block):
        return (
            block.reshape(showers, local_length, HEADS, head_dim)
            .transpose(0, 2, 1, 3)
            .reshape(devices, pairs_here, local_length, head_dim)
        )

    valid_slots = slot_positions < counts[:, None]
    slot_flags = jnp.broadcast_to(
        valid_slots.astype(jnp.bfloat16)[:, None, :], (showers, HEADS, local_length)
    ).reshape(devices, pairs_here, local_length)
    query_rows = lax.all_to_all(to_pairs(queries), "head", split_axis=0, concat_axis=2, tiled=True)
    key_rows = lax.all_to_all(to_pairs(keys), "head", split_axis=0, concat_axis=2, tiled=True)
    value_rows = lax.all_to_all(to_pairs(values), "head", split_axis=0, concat_axis=2, tiled=True)
    flag_rows = lax.all_to_all(slot_flags, "head", split_axis=0, concat_axis=2, tiled=True)
    pair_count = query_rows.shape[1]
    flag_rows = flag_rows[0]
    attention_part = lax.map(
        attend_pair, (query_rows[0], key_rows[0], value_rows[0], flag_rows > 0.5)
    )
    flag_values = flag_rows.astype(jnp.float32)
    window_count = jnp.sum(flag_values.reshape(pair_count, windows, POOL), axis=2)
    window_sum = jnp.sum(
        attention_part.astype(jnp.float32).reshape(pair_count, windows, POOL, head_dim), axis=2
    )
    pooled_part = (window_sum / jnp.maximum(window_count, 1.0)[:, :, None]).astype(jnp.bfloat16)
    attention, pooled, window_count = (
        attention_part,
        pooled_part,
        window_count.astype(jnp.bfloat16),
    )
    pooled_all, count_all = (
        lax.all_gather(pooled, "head", axis=0, tiled=True),
        lax.all_gather(window_count, "head", axis=0, tiled=True),
    )
    pooled_rows = (
        pooled_all.reshape(showers, HEADS, devices, per_device, head_dim)
        .transpose(2, 0, 3, 1, 4)
        .reshape(devices, showers, per_device, model_width)
        .astype(jnp.float32)
    )
    row_count = (
        count_all.reshape(showers, HEADS, devices, per_device)[:, 0]
        .transpose(1, 0, 2)
        .astype(jnp.float32)
    )
    embedding = sinusoid(timesteps, time_weight.shape[0]).astype(jnp.bfloat16)
    modulation = jnp.dot(embedding, time_weight, preferred_element_type=jnp.float32)
    shifts = modulation[:, None, :model_width]
    scales = 1.0 + modulation[:, None, model_width:]
    inverse_rms = lax.rsqrt(jnp.mean(pooled_rows * pooled_rows, axis=3, keepdims=True) + epsilon)
    unit_rows = pooled_rows * inverse_rms
    normed = (
        (unit_rows * norm_gain * scales[None] + shifts[None])
        .astype(jnp.bfloat16)
        .reshape(row_total, model_width)
    )
    own_pooled = lax.dynamic_slice_in_dim(pooled_rows, device_index, 1, 0)[0]
    own_count = lax.dynamic_slice_in_dim(row_count, device_index, 1, 0)[0]
    own_units = lax.dynamic_slice_in_dim(unit_rows, device_index, 1, 0)[0]
    own_inverse = lax.dynamic_slice_in_dim(inverse_rms, device_index, 1, 0)[0]
    shower_counts = counts.astype(jnp.float32)
    class_matrix = class_weight.astype(jnp.float32)
    target = (
        labels[:, None] == jnp.arange(class_matrix.shape[1], dtype=jnp.int32)[None, :]
    ).astype(jnp.float32)
    gate_out = jnp.dot(normed, gate_weight, preferred_element_type=jnp.float32)
    up_out = jnp.dot(normed, up_weight, preferred_element_type=jnp.float32)
    activated = jax.nn.silu(gate_out)
    hidden = (activated * up_out).astype(jnp.bfloat16)
    own_mlp = lax.psum_scatter(
        jnp.dot(hidden, down_weight, preferred_element_type=jnp.float32),
        "head",
        scatter_dimension=0,
        tiled=True,
    ).reshape(showers, per_device, model_width)
    partial_value = jnp.sum(own_count[:, :, None] * (own_pooled + own_mlp), axis=1)
    features = lax.psum(partial_value, "head") / shower_counts[:, None]
    logits = jnp.dot(features, class_matrix, precision=lax.Precision.HIGHEST) + class_bias
    exponent = jnp.exp(logits - jnp.max(logits, axis=1, keepdims=True))
    probability = exponent / jnp.sum(exponent, axis=1, keepdims=True)
    feature_grad = jnp.dot(target - probability, class_matrix.T, precision=lax.Precision.HIGHEST)
    row_grads = (
        row_count[:, :, :, None]
        / shower_counts[None, :, None, None]
        * feature_grad[None, :, None, :]
    )
    hidden_grad = jnp.dot(
        row_grads.astype(jnp.bfloat16).reshape(row_total, model_width),
        down_weight.T,
        preferred_element_type=jnp.float32,
    )
    sigmoid_gate = jax.nn.sigmoid(gate_out)
    gate_grad = (
        hidden_grad * up_out * sigmoid_gate * (1.0 + gate_out * (1.0 - sigmoid_gate))
    ).astype(jnp.bfloat16)
    up_grad = (hidden_grad * activated).astype(jnp.bfloat16)
    normed_grad = lax.psum_scatter(
        jnp.dot(gate_grad, gate_weight.T, preferred_element_type=jnp.float32)
        + jnp.dot(up_grad, up_weight.T, preferred_element_type=jnp.float32),
        "head",
        scatter_dimension=0,
        tiled=True,
    ).reshape(showers, per_device, model_width)
    own_row_grads = lax.dynamic_slice_in_dim(row_grads, device_index, 1, 0)[0]
    unit_grad = normed_grad * norm_gain * scales
    pooled_grad = own_inverse * (
        unit_grad - own_units * jnp.mean(unit_grad * own_units, axis=2, keepdims=True)
    )
    guidance = windows * (own_row_grads + pooled_grad)
    return (attention, guidance)


def solution(mesh):
    in_specs = (
        P("parts", "head", None),
        P("parts", "head", None),
        P("parts", "head", None),
        P("parts", "head"),
        P("parts"),
        P("parts"),
        P("parts"),
        P(),
        P(),
        P(None, "head"),
        P(None, "head"),
        P("head", None),
        P(),
        P(),
    )
    out_specs = (P(("parts", "head"), None, None), P("parts", "head", None))
    return jax.shard_map(body, mesh=mesh, in_specs=in_specs, out_specs=out_specs, check_vma=False)
```

profile of v0, /device:TPU:0, one launch (start us, length us, event | category | flops | bytes accessed | tf_op | source)
XLA Modules:
  0.0 928.7 jit_solution(15136962674087946436)
XLA Ops:
  8.8 7.3 all-to-all-start
  16.2 7.1 reshape.154
  23.3 5.8 copy.119
  29.0 7.9 reshape.178
  36.9 6.0 all-to-all-start.1
  42.9 7.1 reshape.156
  50.0 5.7 copy.121
  55.7 7.9 reshape.180
  63.6 28.0 %all-to-all-done.1 = bf16[32,2,16384]{2,1,0:T(2,128)(2,1)} async-done(((bf16[32,2,16384]{2,1,0:T(2,128)(2,1)}), bf16[32,2,16384]{2,1,0:T(2,128)(2,1)}, u32[]{:S(2)}, u32[]{:S(2)}) %all-to-all-start.1) | async-done | bytes 2097184 | tf_op jit(solution)/shard_map/all_to_all | solution.py:72
  91.6 4.7 all-to-all-start.2
  96.4 7.1 reshape.158
  103.4 5.7 copy.123
  109.2 7.9 reshape.182
  117.0 28.0 %all-to-all-done.2 = bf16[32,2,16384]{2,1,0:T(2,128)(2,1)} async-done(((bf16[32,2,16384]{2,1,0:T(2,128)(2,1)}), bf16[32,2,16384]{2,1,0:T(2,128)(2,1)}, u32[]{:S(2)}, u32[]{:S(2)}) %all-to-all-start.2) | async-done | bytes 2097184 | tf_op jit(solution)/shard_map/all_to_all | solution.py:73
  145.1 4.2 all-to-all-start.3
  150.7 7.9 reshape.179
  158.6 5.5 copy.144
  164.1 7.9 reshape.181
  172.1 5.5 copy.145
  177.6 20.4 %all-to-all-done.3 = bf16[32,2,16384]{2,1,0:T(2,128)(2,1)} async-done(((bf16[32,2,16384]{2,1,0:T(2,128)(2,1)}), bf16[32,2,16384]{2,1,0:T(2,128)(2,1)}, u32[]{:S(2)}, u32[]{:S(2)}) %all-to-all-start.3) | async-done | bytes 2097184 | tf_op jit(solution)/shard_map/all_to_all | solution.py:74
  198.0 7.9 reshape.183
  205.9 5.5 copy.146
  211.5 119.1 %while.10 = (s32[]{:T(128)}, bf16[8,2048,64]{1,2,0:T(8,128)(2,1)}, pred[8,2048]{1,0:T(8,128)(4,1)S(1)}, bf16[8,2048,64]{2,1,0:T(8,128)(2,1)}, bf16[8,2048,64]{2,...) while((s32[]{:T(128)}, bf16[8,2048,64]{1,2,0:T(8,128)(2,1)}, pred[8,2048]{1,0:T(8,128)(4,1)S(1)}, ...), condition=%wide.region_3.4_spmd, body=%wide.region_0.3_spmd.sunk | while | flops 1124333568 | bytes 52238416 | solution.py:78
  215.4 5.0 fusion.76
  220.5 6.0 fusion.77
  226.5 3.7 fusion.75
  230.3 5.0 fusion.76
  235.3 6.0 fusion.77
  241.4 3.7 fusion.75
  245.1 5.0 fusion.76
  250.2 6.0 fusion.77
  256.3 3.7 fusion.75
  260.0 5.0 fusion.76
  265.1 6.0 fusion.77
  274.9 5.0 fusion.76
  279.9 6.0 fusion.77
  289.8 5.0 fusion.76
  294.8 6.0 fusion.77
  304.6 5.0 fusion.76
  309.7 6.0 fusion.77
  319.5 5.0 fusion.76
  324.6 6.0 fusion.77
  330.6 5.7 copy.133
  336.3 5.4 bitcast_reduce_fusion
  343.4 5.3 mul.174
  348.8 10.2 %mul.175 = f32[1024,2048]{1,0:T(8,128)} reshape(f32[32,8,4,2048]{3,2,1,0:T(4,128)} %mul.174) | data formatting | bytes 16777216 | tf_op jit(solution)/shard_map/mul | solution.py:114
  359.0 5.3 add.82
  364.3 10.0 %add.83 = f32[1024,2048]{1,0:T(8,128)} reshape(f32[32,8,4,2048]{3,2,1,0:T(4,128)} %add.82) | data formatting | bytes 16777216 | tf_op jit(solution)/shard_map/add | solution.py:114
  374.3 29.9 %all-gather.2.cloned.1.call-done = bf16[256,128,64]{1,2,0:T(8,128)(2,1)} async-done(((bf16[8,128,64]{1,2,0:T(8,128)(2,1)}), bf16[256,128,64]{1,2,0:T(8,128)(2,1)}) %all-gather.2.cloned.1.call-update) | async-done | bytes 4194320 | tf_op jit(solution)/shard_map/all_gather | solution.py:93
  404.2 4.0 multiply_reduce_fusion
  409.8 12.7 %copy.135 = f32[256,128,64]{2,0,1:T(8,128)} copy(bf16[256,128,64]{1,2,0:T(8,128)(2,1)} %all-gather.2.cloned.1.call-done) | data formatting | bytes 12582912 | tf_op jit(solution)/shard_map/convert_element_type | solution.py:100
  422.5 11.9 %copy.137 = f32[32,8,4,32,64]{4,3,2,1,0:T(8,128)} copy(f32[32,8,4,32,64]{4,3,1,2,0:T(8,128)} %bitcast.115) | data formatting | bytes 16777216 | tf_op jit(solution)/shard_map/convert_element_type | solution.py:100
  434.4 14.8 %reshape.169 = f32[1024,2048]{1,0:T(8,128)} reshape(f32[32,8,4,32,64]{4,3,2,1,0:T(8,128)} %copy.137) | data formatting | bytes 16777216 | tf_op jit(solution)/shard_map/convert_element_type | solution.py:100
  449.2 10.5 %add_convert_fusion = bf16[1024,2048]{1,0:T(8,128)(2,1)S(1)} fusion(f32[1024,2048]{1,0:T(8,128)} %add.83, f32[1024,2048]{1,0:T(8,128)} %mul.175, f32[1024,2048]{1,0:T(8,128)} %reshape.169, f32[2048]{0:T(1024)S(1)} %copy-done.8, f32[1024]{0:T(1024)S(1)} %rsqrt.18), kind=kLoop, calls=%fused_computation.24 | loop fusion | flops 10485760 | bytes 29372416 | tf_op jit(solution)/shard_map/convert_element_type | solution.py:115
  463.2 4.5 fusion.21
  467.8 39.8 %all_gather.6 = bf16[256,128]{1,0:T(8,128)(2,1)S(1)} all-gather(bf16[8,128]{1,0:T(8,128)(2,1)S(1)} %copy-done.10), channel_id=1, replica_groups=mesh['parts'=1,'head'=32] {'head'}, dimensions={0}, use_global_device_ids=true | all-gather | bytes 67584 | tf_op jit(solution)/shard_map/all_gather | solution.py:94
  513.1 14.9 %reshape.168 = f32[32,8,4,2048]{3,1,2,0:T(8,128)} reshape(f32[32,8,4,32,64]{4,3,1,2,0:T(8,128)} %bitcast.116) | data formatting | bytes 16777216 | tf_op jit(solution)/shard_map/convert_element_type | solution.py:100
  529.7 87.3 %reduce-scatter.3.cloned.1.call-done = f32[32,2048]{1,0:T(8,128)} async-done(((f32[1024,2048]{1,0:T(8,128)}), f32[32,2048]{1,0:T(8,128)}) %reduce-scatter.3.cloned.1.call-update) | async-done | bytes 262160 | tf_op jit(solution)/shard_map/reduce_scatter | solution.py:131
  623.3 114.5 %all-reduce.2.cloned.1.call-done = f32[8,2048]{1,0:T(8,128)} async-done(((f32[8,2048]{1,0:T(8,128)}), f32[8,2048]{1,0:T(8,128)}) %all-reduce.2.cloned.1.call-update) | async-done | bytes 65552 | tf_op jit(solution)/shard_map/psum | solution.py:138
  741.1 5.4 mul.180
  746.5 10.3 %mul.186 = f32[1024,2048]{1,0:T(8,128)} reshape(f32[32,8,4,2048]{3,2,1,0:T(4,128)} %mul.180) | data formatting | bytes 16777216 | tf_op jit(solution)/shard_map/mul | solution.py:144
  756.8 5.1 fusion.18
  763.4 4.6 convolution_add_fusion
  769.5 149.8 %reduce-scatter.5.cloned.1.call-done = f32[32,2048]{1,0:T(8,128)} async-done(((f32[1024,2048]{1,0:T(8,128)}), f32[32,2048]{1,0:T(8,128)}) %reduce-scatter.5.cloned.1.call-update) | async-done | bytes 262160 | tf_op jit(solution)/shard_map/reduce_scatter | solution.py:158
  (110 shorter events, 51.0 us)
Async XLA Ops:
  7.2 335.9 %copy-start = (bf16[256,4096]{1,0:T(8,128)(2,1)S(1)}, bf16[256,4096]{1,0:T(8,128)(2,1)}, u32[]{:S(2)}) copy-start(bf16[256,4096]{1,0:T(8,128)(2,1)} %param.23) | copy-start | bytes 6291460
  8.8 28.1 %all-to-all-start = ((bf16[32,2,256]{2,1,0:T(2,128)(2,1)}), bf16[32,2,256]{2,1,0:T(2,128)(2,1)S(1)}, u32[]{:S(2)}, u32[]{:S(2)}) async-start(bf16[32,2,256]{2,1,0:T(2,128)(2,1)} %reshape.176), calls=%async_computation | async-start | bytes 65536 | tf_op jit(solution)/shard_map/all_to_all | solution.py:75
  36.9 54.7 %all-to-all-start.1 = ((bf16[32,2,16384]{2,1,0:T(2,128)(2,1)}), bf16[32,2,16384]{2,1,0:T(2,128)(2,1)}, u32[]{:S(2)}, u32[]{:S(2)}) async-start(bf16[32,2,16384]{2,1,0:T(2,128)(2,1)} %reshape.178), calls=%async_computation.1 | async-start | bytes 4194304 | tf_op jit(solution)/shard_map/all_to_all | solution.py:72
  91.6 53.5 %all-to-all-start.2 = ((bf16[32,2,16384]{2,1,0:T(2,128)(2,1)}), bf16[32,2,16384]{2,1,0:T(2,128)(2,1)}, u32[]{:S(2)}, u32[]{:S(2)}) async-start(bf16[32,2,16384]{2,1,0:T(2,128)(2,1)} %reshape.180), calls=%async_computation.2 | async-start | bytes 4194304 | tf_op jit(solution)/shard_map/all_to_all | solution.py:73
  145.1 52.9 %all-to-all-start.3 = ((bf16[32,2,16384]{2,1,0:T(2,128)(2,1)}), bf16[32,2,16384]{2,1,0:T(2,128)(2,1)}, u32[]{:S(2)}, u32[]{:S(2)}) async-start(bf16[32,2,16384]{2,1,0:T(2,128)(2,1)} %reshape.182), calls=%async_computation.3 | async-start | bytes 4194304 | tf_op jit(solution)/shard_map/all_to_all | solution.py:74
  149.3 254.9 %all-gather.2.cloned.1.call-start = ((), (), s32[]{:S(2)}) async-start(), calls=%async_computation.6 | async-start | bytes 4325376 | tf_op jit(solution)/shard_map/all_gather | solution.py:93
  330.6 11.2 %copy-start.9 = (f32[8,128]{1,0:T(8,128)S(1)}, f32[8,128]{1,0:T(8,128)}, u32[]{:S(2)}) copy-start(f32[8,128]{1,0:T(8,128)} %get-tuple-element.86) | copy-start | bytes 12292
  330.6 12.3 %copy-start.12 = (s32[8]{0:T(128)S(1)}, s32[8]{0:T(128)}, u32[]{:S(2)}) copy-start(s32[8]{0:T(128)} %param.21) | copy-start | bytes 100
  342.8 274.1 %reduce-scatter.3.cloned.1.call-start = ((), (), s32[]{:S(2)}) async-start(), calls=%async_computation.7 | async-start | bytes 8650752 | tf_op jit(solution)/shard_map/reduce_scatter | solution.py:131
  434.4 14.8 %copy-start.8 = (f32[2048]{0:T(1024)S(1)}, f32[2048]{0:T(1024)}, u32[]{:S(2)}) copy-start(f32[2048]{0:T(1024)} %param.24) | copy-start | bytes 24580
  449.2 10.5 %copy-start.4 = (bf16[2048,256]{1,0:T(8,128)(2,1)S(1)}, bf16[2048,256]{1,0:T(8,128)(2,1)}, u32[]{:S(2)}) copy-start(bf16[2048,256]{1,0:T(8,128)(2,1)} %param.25) | copy-start | bytes 3145732
  449.2 11.8 %copy-start.6 = (bf16[2048,256]{1,0:T(8,128)(2,1)S(1)}, bf16[2048,256]{1,0:T(8,128)(2,1)}, u32[]{:S(2)}) copy-start(bf16[2048,256]{1,0:T(8,128)(2,1)} %param.26) | copy-start | bytes 3145732
  459.7 3.5 copy-start.3
  462.2 1.0 copy-start.1
  463.2 4.6 copy-start.11
  463.2 4.6 copy-start.10
  467.7 270.1 %all-reduce.2.cloned.1.call-start = ((), (), s32[]{:S(2)}) async-start(), calls=%async_computation.8 | async-start | bytes 131072 | tf_op jit(solution)/shard_map/psum | solution.py:138
  620.6 298.6 %reduce-scatter.5.cloned.1.call-start = ((), (), s32[]{:S(2)}) async-start(), calls=%async_computation.9 | async-start | bytes 8650752 | tf_op jit(solution)/shard_map/reduce_scatter | solution.py:158
  756.8 5.1 copy-start.2
  756.8 5.1 copy-start.5
  761.9 1.5 copy-start.7
Sparse Core Ops, SparseCore 0:
  342.9 61.2 all-gather.1
  467.9 149.0 reduce-scatter.2
  622.5 115.2 all-reduce.1
  768.2 151.0 reduce-scatter.4
where the time goes:
time: 940 us; the launch traced here: 929 us
  waiting for transfers between devices  458 us (49%)
  local copies, waits for them, and re-layouts  224 us (24%)
  matrix products  99.8 us (11%)
  other arithmetic  70.2 us (7%)
  blocking collectives  39.8 us (4%)
  starting transfers between devices  22.4 us (2%)
  between operations  14.6 us (2%)
    reduce_scatter x1, waiting for transfers between devices, body(): lax.psum_scatter(jnp.dot(gate_grad, gate_weight.T, preferred_element_type...  150 us
    psum x1, waiting for transfers between devices, body(): features = lax.psum(partial_value, 'head') / shower_counts[:, None]  115 us
    reduce_scatter x1, waiting for transfers between devices, body(): lax.psum_scatter(jnp.dot(hidden, down_weight, preferred_element_type=jnp....  87.3 us
    convert_element_type x4, local copies, waits for them, and re-layouts, body(): pooled_rows = pooled_all.reshape(showers, HEADS, devices, per_device, hea...  54.3 us
    unnamed x34, local copies, waits for them, and re-layouts  49.3 us
    dot_general x8, matrix products, attend_pair(): mixed = jnp.dot(weights, value_rows, preferred_element_type=jnp.float32)  48.2 us
    reduce_sum x8, other arithmetic, attend_pair(): jnp.sum(exponent, axis=1, keepdims=True)  40.4 us
    all_gather x1, blocking collectives, body(): lax.all_gather(window_count, 'head', axis=0, tiled=True)  39.8 us
  transfers between devices with their start and end apart: 8, of which 7 were waited for; matrix products, arithmetic and copies ran while one was open for 16% of the time, Pallas kernels for 0%

commit v1 on v0

v1 whole, which is shorter than its diff:
```python
import functools
import math

import jax
import jax.numpy as jnp
from jax import lax
from jax.experimental import pallas as pl
from jax.experimental.pallas import tpu as pltpu
from jax.sharding import PartitionSpec as P

HEADS = 32
POOL = 16
QTILE = 256
MESH = pl.DeviceIdType.MESH

epsilon = 1e-06
HIGHEST = lax.Precision.HIGHEST


def sinusoid(steps, embed_width):
    half_width = embed_width // 2
    frequency = jnp.exp(-math.log(10000.0) * jnp.arange(half_width, dtype=jnp.float32) / half_width)
    angles = steps.astype(jnp.float32)[:, None] * frequency[None, :]
    return jnp.concatenate([jnp.cos(angles), jnp.sin(angles)], axis=1)


def greet_all(n, me):
    barrier = pltpu.get_barrier_semaphore()

    def greet(k, carry):
        pl.semaphore_signal(
            barrier, inc=1, device_id={"head": lax.rem(me + k, n)}, device_id_type=MESH
        )
        return carry

    lax.fori_loop(1, n, greet, 0)
    pl.semaphore_wait(barrier, n - 1)


def swap_kernel(n, q, k, v, f, qo, ko, vo, fo, send_sem, recv_sem, own_sem):
    me = lax.axis_index("head")
    showers, rows, width = q.shape
    cols = qo.shape[1]
    groups = width // cols
    fields = ((q, qo), (k, ko), (v, vo))
    greet_all(n, me)

    def block_of(field, dst):
        return field.at[dst // groups, :, pl.ds(pl.multiple_of((dst % groups) * cols, cols), cols)]

    def slot_of(out, src):
        return out.at[pl.ds(pl.multiple_of(src * rows, rows), rows), :]

    own = [
        pltpu.make_async_copy(block_of(a, me), slot_of(o, me), own_sem.at[i])
        for i, (a, o) in enumerate(fields)
    ]
    own.append(pltpu.make_async_copy(f, fo.at[me], own_sem.at[3]))
    for copy in own:
        copy.start()

    def copies(step):
        dst = lax.rem(me + step, n)
        result = [
            pltpu.make_async_remote_copy(
                src_ref=f,
                dst_ref=fo.at[me],
                send_sem=send_sem.at[3, step],
                recv_sem=recv_sem.at[3, step],
                device_id={"head": dst},
                device_id_type=MESH,
            )
        ]
        for i, (a, o) in enumerate(fields):
            result.append(
                pltpu.make_async_remote_copy(
                    src_ref=block_of(a, dst),
                    dst_ref=slot_of(o, me),
                    send_sem=send_sem.at[i, step],
                    recv_sem=recv_sem.at[i, step],
                    device_id={"head": dst},
                    device_id_type=MESH,
                )
            )
        return result

    def begin(step, carry):
        for copy in copies(step):
            copy.start()
        return carry

    def finish(step, carry):
        for copy in copies(step):
            copy.wait()
        return carry

    lax.fori_loop(1, n, begin, 0)
    lax.fori_loop(1, n, finish, 0)
    for copy in own:
        copy.wait()


def swap(n, q, k, v, f, cols):
    rows = q.shape[1]
    field = jax.ShapeDtypeStruct((n * rows, cols), q.dtype)
    return pl.pallas_call(
        functools.partial(swap_kernel, n),
        out_shape=(field, field, field, jax.ShapeDtypeStruct((n,) + f.shape, f.dtype)),
        in_specs=[pl.BlockSpec(memory_space=pl.ANY)] * 4,
        out_specs=[pl.BlockSpec(memory_space=pl.ANY)] * 4,
        scratch_shapes=[
            pltpu.SemaphoreType.DMA((4, n)),
            pltpu.SemaphoreType.DMA((4, n)),
            pltpu.SemaphoreType.DMA((4,)),
        ],
        compiler_params=pltpu.CompilerParams(collective_id=1, has_side_effects=True),
    )(q, k, v, f)


def total_kernel(n, x, out, held, send_sem, recv_sem):
    me = lax.axis_index("head")
    greet_all(n, me)

    def copy_of(step):
        return pltpu.make_async_remote_copy(
            src_ref=x,
            dst_ref=held.at[step],
            send_sem=send_sem.at[step],
            recv_sem=recv_sem.at[step],
            device_id={"head": lax.rem(me + step, n)},
            device_id_type=MESH,
        )

    def begin(step, carry):
        copy_of(step).start()
        return carry

    def finish(step, carry):
        copy_of(step).wait()
        return carry

    held[0] = x[...]
    lax.fori_loop(1, n, begin, 0)
    lax.fori_loop(1, n, finish, 0)
    total = jnp.zeros(out.shape, jnp.float32)
    for source in range(n):
        total = total + held[lax.rem(me - source + n, n)]
    out[...] = total


def total_over(n, x):
    return pl.pallas_call(
        functools.partial(total_kernel, n),
        out_shape=jax.ShapeDtypeStruct(x.shape, jnp.float32),
        in_specs=[pl.BlockSpec(memory_space=pltpu.VMEM)],
        out_specs=pl.BlockSpec(memory_space=pltpu.VMEM),
        scratch_shapes=[
            pltpu.VMEM((n,) + x.shape, jnp.float32),
            pltpu.SemaphoreType.DMA((n,)),
            pltpu.SemaphoreType.DMA((n,)),
        ],
        compiler_params=pltpu.CompilerParams(collective_id=2, has_side_effects=True),
    )(x)


def scatter_plan(n, orders):
    plan = []
    for order in orders:
        stages = []
        kept = list(range(n))
        for position, bit in enumerate(order):
            away = [r for r in kept if (r >> bit) & 1]
            kept = [r for r in kept if not (r >> bit) & 1]
            following = order[position + 1] if position + 1 < len(order) else None
            if following is not None:
                kept.sort(key=lambda r: (1 - ((r >> following) & 1), r))
            away = [r ^ (1 << bit) for r in kept]
            away = [r for r in away]
            stages.append((bit, away, list(kept)))
        plan.append(stages)
    return plan


def reduce_kernel(n, plan, x, out, held, send_sem, recv_sem):
    me = lax.axis_index("head")
    bits = n.bit_length() - 1
    width = x.shape[2] // len(plan)
    bit_of = [(me // (1 << b)) % 2 for b in range(bits)]

    def flipped(r):
        result = me
        for b in range(bits):
            if (r >> b) & 1:
                result = result + (1 << b) * (1 - 2 * bit_of[b])
        return result

    barrier = pltpu.get_barrier_semaphore()
    for b in range(bits):
        pl.semaphore_signal(
            barrier, inc=1, device_id={"head": flipped(1 << b)}, device_id_type=MESH
        )
    pl.semaphore_wait(barrier, bits)

    def copy_of(stream, slot, bit, r):
        columns = pl.ds(stream * width, width)
        return pltpu.make_async_remote_copy(
            src_ref=x.at[flipped(r), :, columns],
            dst_ref=held.at[stream, slot],
            send_sem=send_sem.at[stream, slot],
            recv_sem=recv_sem.at[stream, slot],
            device_id={"head": flipped(1 << bit)},
            device_id_type=MESH,
        )

    stage_count = len(plan[0])
    slots = [0]
    for stage in range(stage_count):
        slots.append(slots[-1] + len(plan[0][stage][1]))
    everything = []
    for i in range(len(plan[0][0][1])):
        for stream, stages in enumerate(plan):
            bit, away, kept = stages[0]
            copy = copy_of(stream, i, bit, away[i])
            copy.start()
            everything.append(copy)
    for stage in range(stage_count):
        for i in range(len(plan[0][stage][1])):
            for stream, stages in enumerate(plan):
                bit, away, kept = stages[stage]
                slot = slots[stage] + i
                copy_of(stream, slot, bit, away[i]).wait_recv()
                columns = pl.ds(stream * width, width)
                chunk = flipped(kept[i])
                value = x[chunk, :, columns].astype(jnp.float32) + held[stream, slot].astype(
                    jnp.float32
                )
                if stage == stage_count - 1:
                    out[:, columns] = value
                    continue
                x[chunk, :, columns] = value.astype(jnp.bfloat16)
                next_bit, next_away, _ = stages[stage + 1]
                if kept[i] in next_away:
                    copy = copy_of(
                        stream,
                        slots[stage + 1] + next_away.index(kept[i]),
                        next_bit,
                        kept[i],
                    )
                    copy.start()
                    everything.append(copy)
    for copy in everything:
        copy.wait_send()


def reduce_kernel_entry(n, plan, x_ref, out, x, held, load_sem, send_sem, recv_sem):
    load = pltpu.make_async_copy(x_ref, x, load_sem)
    load.start()
    load.wait()
    reduce_kernel(n, plan, x, out, held, send_sem, recv_sem)


def reduce_over(n, x, orders):
    plan = scatter_plan(n, orders)
    chunks, rows, columns = x.shape
    streams = len(plan)
    return pl.pallas_call(
        functools.partial(reduce_kernel_entry, n, plan),
        out_shape=jax.ShapeDtypeStruct((rows, columns), jnp.float32),
        in_specs=[pl.BlockSpec(memory_space=pl.ANY)],
        out_specs=pl.BlockSpec(memory_space=pltpu.VMEM),
        scratch_shapes=[
            pltpu.VMEM(x.shape, x.dtype),
            pltpu.VMEM((streams, n, rows, columns // streams), x.dtype),
            pltpu.SemaphoreType.DMA,
            pltpu.SemaphoreType.DMA((streams, n)),
            pltpu.SemaphoreType.DMA((streams, n)),
        ],
        compiler_params=pltpu.CompilerParams(
            collective_id=3, has_side_effects=True, vmem_limit_bytes=40 * 1024 * 1024
        ),
    )(x)


def attend_kernel(head_dim, q_ref, k_ref, v_ref, valid_ref, att_ref, pooled_ref, key_scratch):
    tile = pl.program_id(1)
    lanes = q_ref.shape[1]
    heads = lanes // head_dim
    length = k_ref.shape[0]
    qtile = q_ref.shape[0]
    key_lane = lax.broadcasted_iota(jnp.int32, (length, lanes), 1)
    lane = lax.broadcasted_iota(jnp.int32, (qtile, lanes), 1)

    @pl.when(tile == 0)
    def _():
        bias = jnp.where(valid_ref[...] > 0.5, 0.0, -1e30)
        for h in range(heads):
            spare = ((h + 1) % heads) * head_dim
            key_scratch[h] = jnp.where(
                key_lane == spare, bias, k_ref[...].astype(jnp.float32)
            ).astype(jnp.bfloat16)

    valid = valid_ref[pl.ds(pl.multiple_of(tile * qtile, qtile), qtile), :]
    query = q_ref[...].astype(jnp.float32) * head_dim ** (-0.5)
    mixed = []
    for h in range(heads):
        spare = ((h + 1) % heads) * head_dim
        inside = (lane >= h * head_dim) & (lane < (h + 1) * head_dim)
        own = jnp.where(inside, query, jnp.where(lane == spare, 1.0, 0.0)).astype(jnp.bfloat16)
        scores = lax.dot_general(
            own, key_scratch[h], (((1,), (1,)), ((), ())), preferred_element_type=jnp.float32
        )
        peak = jnp.max(scores, axis=1, keepdims=True)
        exponent = jnp.exp(scores - peak)
        weights = (exponent * (1.0 / jnp.sum(exponent, axis=1, keepdims=True))).astype(
            jnp.bfloat16
        )
        result = jnp.dot(weights, v_ref[...], preferred_element_type=jnp.float32)
        result = result * valid
        mixed.append(result)
        att_ref[h] = result[:, h * head_dim : (h + 1) * head_dim].astype(jnp.bfloat16)
    joined = mixed[0]
    for h in range(1, heads):
        joined = jnp.where(lane >= h * head_dim, mixed[h], joined)
    windows = qtile // POOL
    row = lax.broadcasted_iota(jnp.int32, (windows, qtile), 0)
    slot = lax.broadcasted_iota(jnp.int32, (windows, qtile), 1)
    gather = jnp.where(slot // POOL == row, 1.0, 0.0).astype(jnp.bfloat16)
    sums = jnp.dot(gather, joined.astype(jnp.bfloat16), preferred_element_type=jnp.float32)
    count = jnp.dot(gather, valid.astype(jnp.bfloat16), preferred_element_type=jnp.float32)
    pooled_ref[...] = (sums / jnp.maximum(count, 1.0)).astype(jnp.bfloat16)


def attend(q, k, v, valid, head_dim):
    length, cols = q.shape
    lanes = 2 * head_dim
    heads = cols // head_dim
    qtile = min(QTILE, length)
    return pl.pallas_call(
        functools.partial(attend_kernel, head_dim),
        grid=(cols // lanes, length // qtile),
        out_shape=(
            jax.ShapeDtypeStruct((heads, length, head_dim), jnp.bfloat16),
            jax.ShapeDtypeStruct((length // POOL, cols), jnp.bfloat16),
        ),
        in_specs=[
            pl.BlockSpec((qtile, lanes), lambda p, t: (t, p)),
            pl.BlockSpec((length, lanes), lambda p, t: (0, p)),
            pl.BlockSpec((length, lanes), lambda p, t: (0, p)),
            pl.BlockSpec((length, lanes), lambda p, t: (0, 0)),
        ],
        out_specs=[
            pl.BlockSpec((2, qtile, head_dim), lambda p, t: (p, t, 0)),
            pl.BlockSpec((qtile // POOL, lanes), lambda p, t: (t, p)),
        ],
        scratch_shapes=[pltpu.VMEM((2, length, lanes), jnp.bfloat16)],
        compiler_params=pltpu.CompilerParams(
            dimension_semantics=("arbitrary", "arbitrary"), vmem_limit_bytes=48 * 1024 * 1024
        ),
    )(q, k, v, valid)


def body(
    queries,
    keys,
    values,
    slot_positions,
    counts,
    timesteps,
    labels,
    time_weight,
    norm_gain,
    gate_weight,
    up_weight,
    down_weight,
    class_weight,
    class_bias,
):
    devices = lax.axis_size("head")
    device_index = lax.axis_index("head")
    showers, local_length, model_width = queries.shape
    head_dim = model_width // HEADS
    pairs_here = showers * HEADS // devices
    length = local_length * devices
    windows = length // POOL
    per_device = windows // devices
    row_total = showers * windows
    cols = pairs_here * head_dim
    groups = model_width // cols

    padded = -(-local_length // 128) * 128
    positions = jnp.pad(slot_positions, ((0, 0), (0, padded - local_length)))
    query_rows, key_rows, value_rows, position_rows = swap(
        devices, queries, keys, values, positions, cols
    )
    valid_all = (position_rows[:, :, :local_length] < counts[None, :, None]).astype(jnp.float32)
    own_shower = device_index // groups
    own_valid = lax.dynamic_index_in_dim(valid_all, own_shower, 1, keepdims=False).reshape(length)
    attention, pooled = attend(
        query_rows,
        key_rows,
        value_rows,
        jnp.broadcast_to(own_valid[:, None], (length, 2 * head_dim)),
        head_dim,
    )
    row_count = jnp.sum(valid_all.reshape(devices, showers, per_device, POOL), axis=3)
    pooled_all = lax.all_gather(pooled, "head", axis=0, tiled=False)
    by_shower = (
        pooled_all.reshape(showers, groups, windows, cols)
        .transpose(0, 2, 1, 3)
        .reshape(row_total, model_width)
    )
    row_id = jnp.arange(row_total, dtype=jnp.int32)
    owner = row_id // (showers * per_device)
    shower_of = (row_id // per_device) % showers
    source = shower_of * windows + owner * per_device + row_id % per_device
    order = (source[:, None] == row_id[None, :]).astype(jnp.bfloat16)
    pooled_rows = jnp.dot(order, by_shower, preferred_element_type=jnp.float32)
    in_shower = shower_of[:, None] == jnp.arange(showers, dtype=jnp.int32)[None, :]
    flat_count = row_count.reshape(row_total)
    spread = in_shower.astype(jnp.float32)

    embedding = sinusoid(timesteps, time_weight.shape[0]).astype(jnp.bfloat16)
    modulation = jnp.dot(embedding, time_weight, preferred_element_type=jnp.float32)
    shifts = modulation[None, :, None, :model_width]
    scales = 1.0 + modulation[:, model_width:]
    gains = norm_gain * scales
    inverse_rms = lax.rsqrt(jnp.mean(pooled_rows * pooled_rows, axis=1, keepdims=True) + epsilon)

    def by_row(table):
        wide = jnp.broadcast_to(
            table[None, :, None, :], (devices, showers, per_device, table.shape[1])
        )
        return wide.reshape(row_total, table.shape[1])

    unit_rows = pooled_rows * inverse_rms
    normed = (
        unit_rows * norm_gain * by_row(scales) + by_row(modulation[:, :model_width])
    ).astype(jnp.bfloat16)
    shower_counts = counts.astype(jnp.float32)
    class_matrix = class_weight.astype(jnp.float32)
    target = (
        labels[:, None] == jnp.arange(class_matrix.shape[1], dtype=jnp.int32)[None, :]
    ).astype(jnp.float32)
    gate_out = jnp.dot(normed, gate_weight, preferred_element_type=jnp.float32)
    up_out = jnp.dot(normed, up_weight, preferred_element_type=jnp.float32)
    activated = jax.nn.silu(gate_out)
    hidden = (activated * up_out).astype(jnp.bfloat16)
    weigh = (spread * flat_count[:, None]).astype(jnp.bfloat16)
    hidden_sum = lax.dot_general(
        weigh, hidden, (((0,), (0,)), ((), ())), preferred_element_type=jnp.float32
    )
    pooled_sum = lax.dot_general(
        weigh,
        pooled_rows.astype(jnp.bfloat16),
        (((0,), (0,)), ((), ())),
        preferred_element_type=jnp.float32,
    )
    mlp_sum = jnp.dot(hidden_sum, down_weight.astype(jnp.float32), precision=HIGHEST)
    partial_logits = jnp.dot(mlp_sum, class_matrix, precision=HIGHEST)
    logit_sum = total_over(devices, partial_logits) + jnp.dot(
        pooled_sum, class_matrix, precision=HIGHEST
    )
    logits = logit_sum / shower_counts[:, None] + class_bias
    exponent = jnp.exp(logits - jnp.max(logits, axis=1, keepdims=True))
    probability = exponent / jnp.sum(exponent, axis=1, keepdims=True)
    feature_grad = jnp.dot(target - probability, class_matrix.T, precision=HIGHEST)
    row_share = row_count / shower_counts[None, :, None]
    row_grads = (row_share[:, :, :, None] * feature_grad[None, :, None, :]).reshape(
        row_total, model_width
    )
    hidden_grad = jnp.dot(
        row_grads.astype(jnp.bfloat16), down_weight.T, preferred_element_type=jnp.float32
    )
    sigmoid_gate = jax.nn.sigmoid(gate_out)
    gate_grad = (
        hidden_grad * up_out * sigmoid_gate * (1.0 + gate_out * (1.0 - sigmoid_gate))
    ).astype(jnp.bfloat16)
    up_grad = (hidden_grad * activated).astype(jnp.bfloat16)
    normed_grad = (
        jnp.dot(gate_grad, gate_weight.T, preferred_element_type=jnp.float32)
        + jnp.dot(up_grad, up_weight.T, preferred_element_type=jnp.float32)
    ).astype(jnp.bfloat16)
    bits = devices.bit_length() - 1
    high = list(range(bits - 1, 2, -1))
    rows_here = showers * per_device
    normed_grad = reduce_over(
        devices,
        normed_grad.reshape(devices, rows_here, model_width),
        ([0, 1, 2] + high, [0, 2, 1] + high),
    )

    def own_rows(table):
        return lax.dynamic_slice_in_dim(table, device_index * rows_here, rows_here, 0)

    def shower_rows(table):
        wide = jnp.broadcast_to(table[:, None, :], (showers, per_device, table.shape[1]))
        return wide.reshape(rows_here, table.shape[1])

    own_pooled = own_rows(pooled_rows)
    own_inverse = lax.rsqrt(jnp.mean(own_pooled * own_pooled, axis=1, keepdims=True) + epsilon)
    own_units = own_pooled * own_inverse
    own_share = lax.dynamic_index_in_dim(row_share, device_index, 0, keepdims=False)
    own_row_grads = (own_share[:, :, None] * feature_grad[:, None, :]).reshape(
        rows_here, model_width
    )
    unit_grad = normed_grad * norm_gain * shower_rows(scales)
    pooled_grad = own_inverse * (
        unit_grad - own_units * jnp.mean(unit_grad * own_units, axis=1, keepdims=True)
    )
    guidance = windows * (own_row_grads + pooled_grad)
    return (attention, guidance.reshape(showers, per_device, model_width))


def solution(mesh):
    in_specs = (
        P("parts", "head", None),
        P("parts", "head", None),
        P("parts", "head", None),
        P("parts", "head"),
        P("parts"),
        P("parts"),
        P("parts"),
        P(),
        P(),
        P(None, "head"),
        P(None, "head"),
        P("head", None),
        P(),
        P(),
    )
    out_specs = (P(("parts", "head"), None, None), P("parts", "head", None))
    return jax.shard_map(body, mesh=mesh, in_specs=in_specs, out_specs=out_specs, check_vma=False)
```

time: 940 us -> 448 us (0.48); the launches traced: 929 us -> 447 us
  waiting for transfers between devices: 458 us -> 65.8 us
  Pallas kernels: 0 us -> 260 us
  local copies, waits for them, and re-layouts: 224 us -> 66.7 us
  matrix products: 99.8 us -> 24.2 us
  other arithmetic: 70.2 us -> 15.6 us
  blocking collectives: 39.8 us -> 0 us
  starting transfers between devices: 22.4 us -> 0.04 us
    pallas_call x0 -> x4, Pallas kernels: none -> 260 us  [the longest x1 132 us: swap(): pl.pallas_call(functools.partial(swap_kernel, n), out_shape=(field, field...]
    reduce_scatter x2 -> x0, waiting for transfers between devices: 237 us -> none  [the longest x1 150 us: body(): lax.psum_scatter(jnp.dot(gate_grad, gate_weight.T, preferred_element_type...]
    psum x1 -> x0, waiting for transfers between devices: 115 us -> none  [body(): features = lax.psum(partial_value, 'head') / shower_counts[:, None]]
    all_to_all x4 -> x0, waiting for transfers between devices: 76.4 us -> none  [the longest x1 28 us: body(): lax.all_to_all(to_pairs(keys), 'head', split_axis=0, concat_axis=2, tiled...]
    dot_general x20 -> x8, matrix products: 90.8 us -> 16.1 us  [the longest x1 6.72 us: body(): pooled_rows = jnp.dot(order, by_shower, preferred_element_type=jnp.float32)]
    convert_element_type x8 -> x1, local copies, waits for them, and re-layouts: 57.2 us -> 0.13 us  [body(): (position_rows[:, :, :local_length] < counts[None, :, None]).astype(jnp.f...]
    reduce_sum x14 -> x3, other arithmetic: 52.5 us -> 2.3 us  [the longest x1 1.17 us: body(): jnp.mean(unit_grad * own_units, axis=1, keepdims=True)]
    unnamed x34 -> x45, local copies, waits for them, and re-layouts: 49.3 us -> 8.73 us
  transfers between devices with their start and end apart: 8 -> 1, of which waited for: 7 -> 1; matrix products, arithmetic and copies ran while one was open for 16% -> 8% of each run, Pallas kernels for 0% -> 0%
where the time goes in v1:
time: 448 us; the launch traced here: 447 us
  Pallas kernels  260 us (58%)
  local copies, waits for them, and re-layouts  66.7 us (15%)
  waiting for transfers between devices  65.8 us (15%)
  matrix products  24.2 us (5%)
  other arithmetic  15.6 us (3%)
  between operations  14.4 us (3%)
    pallas_call x1, Pallas kernels, swap(): pl.pallas_call(functools.partial(swap_kernel, n), out_shape=(field, field...  132 us
    pallas_call x1, Pallas kernels, attend(): pl.pallas_call(functools.partial(attend_kernel, head_dim), grid=(cols //...  79.7 us
    all_gather x1, waiting for transfers between devices, body(): pooled_all = lax.all_gather(pooled, 'head', axis=0, tiled=False)  65.8 us
    pallas_call x1, Pallas kernels, reduce_over(): pl.pallas_call(functools.partial(reduce_kernel_entry, n, plan), out_shape...  38.8 us
    reshape x2, local copies, waits for them, and re-layouts, by_row(): return wide.reshape(row_total, table.shape[1])  20 us
    mul x2, local copies, waits for them, and re-layouts, body(): row_share[:, :, :, None] * feature_grad[None, :, None, :]  15.4 us
    broadcast_in_dim x2, local copies, waits for them, and re-layouts, by_row(): jnp.broadcast_to(table[None, :, None, :], (devices, showers, per_device,...  10.7 us
    convert_element_type x1, other arithmetic, body(): normed = (unit_rows * norm_gain * by_row(scales) + by_row(modulation[:, :...  10.7 us
  transfers between devices with their start and end apart: 1, of which 1 were waited for; matrix products, arithmetic and copies ran while one was open for 8% of the time, Pallas kernels for 0%

profile of v1, /device:TPU:0, one launch (start us, length us, event | category | flops | bytes accessed | tf_op | source)
XLA Modules:
  0.0 447.1 jit_solution(13395235474041474144)
XLA Ops:
  7.2 0.0 copy-start
  7.2 0.0 all-gather.3.cloned.1.call-start
  7.2 1.4 pad.4.f
  8.7 132.3 %shard_map.149 = (bf16[2048,512]{1,0:T(8,128)(2,1)}, bf16[2048,512]{1,0:T(8,128)(2,1)}, bf16[2048,512]{1,0:T(8,128)(2,1)}, s32[32,8,128]{2,1,0:T(8,128)}) custom-call(bf16[8,64,2048]{2,1,0:T(8,128)(2,1)} %q.1, bf16[8,64,2048]{2,1,0:T(8,128)(2,1)} %k.1, bf16[8,64,2048]{2,1,0:T(8,128)(2,1)} %v.1, s32[8,128]{1,0:T(8,128)} %pad.4.f), custom_call_target="tpu_custom_call" | custom-call | tf_op jit(solution)/shard_map/pallas_call | solution.py:106
  141.0 0.0 copy-done.16
  141.0 1.0 fusion.22
  142.0 0.1 dynamic-slice_reduce_fusion
  142.1 0.1 broadcast_in_dim.10
  142.1 0.3 broadcast_in_dim.11.valid_ref
  142.5 1.6 copy-done.2
  144.1 1.6 copy-done.3
  145.7 79.7 %shard_map.150 = (bf16[8,2048,64]{2,1,0:T(8,128)(2,1)}, bf16[128,512]{1,0:T(8,128)(2,1)}) custom-call(bf16[2048,512]{1,0:T(8,128)(2,1)S(1)} %copy-done.2, bf16[2048,512]{1,0:T(8,128)(2,1)S(1)} %copy-done.3, bf16[2048,512]{1,0:T(8,128)(2,1)} %get-tuple-element.10.v_ref, f32[2048,128]{1,0:T(8,128)S(1)} %broadcast_in_dim.11.valid_ref), custom_call_target="tpu_custom_call" | custom-call | tf_op jit(solution)/shard_map/pallas_call | solution.py:338
  225.3 0.0 all-gather.3.cloned.1.call-update
  225.4 0.1 copy.20
  225.5 4.8 %copy.24 = bf16[8,2048,64]{1,2,0:T(8,128)(2,1)} copy(bf16[8,2048,64]{2,1,0:T(8,128)(2,1)} %get-tuple-element.18) | data formatting | bytes 4194304
  230.3 0.1 fusion.30
  230.4 0.4 fusion.39
  230.8 5.4 %broadcast_in_dim.13 = f32[32,8,4,2048]{3,2,1,0:T(4,128)} broadcast(f32[8,2048]{1,0:T(8,128)S(1)} %get-tuple-element.21), dimensions={1,3} | broadcast | bytes 8454144 | tf_op jit(solution)/shard_map/broadcast_in_dim | solution.py:430
  236.2 10.0 %reshape.135 = f32[1024,2048]{1,0:T(8,128)} reshape(f32[32,8,4,2048]{3,2,1,0:T(4,128)} %broadcast_in_dim.13) | data formatting | bytes 16777216 | tf_op jit(solution)/shard_map/reshape | solution.py:433
  246.2 5.3 %broadcast_in_dim.12 = f32[32,8,4,2048]{3,2,1,0:T(4,128)} broadcast(f32[8,2048]{1,0:T(8,128)S(1)} %get-tuple-element.20), dimensions={1,3} | broadcast | bytes 8454144 | tf_op jit(solution)/shard_map/broadcast_in_dim | solution.py:430
  251.5 10.0 %reshape.134 = f32[1024,2048]{1,0:T(8,128)} reshape(f32[32,8,4,2048]{3,2,1,0:T(4,128)} %broadcast_in_dim.12) | data formatting | bytes 16777216 | tf_op jit(solution)/shard_map/reshape | solution.py:433
  261.5 0.1 bitcast_reduce_fusion
  261.6 0.1 copy.21
  261.7 0.1 mul.172
  261.9 0.1 reshape.137
  262.0 0.1 div.82.clone
  262.1 0.1 div.98
  262.2 0.2 fusion.23
  262.3 0.1 mul.170
  262.5 65.8 %all-gather.3.cloned.1.call-done = bf16[4096,512]{1,0:T(8,128)(2,1)} async-done(((bf16[128,512]{1,0:T(8,128)(2,1)}), bf16[4096,512]{1,0:T(8,128)(2,1)}) %all-gather.3.cloned.1.call-update) | async-done | bytes 4194320 | tf_op jit(solution)/shard_map/all_gather | solution.py:406
  328.3 7.6 %copy.22 = bf16[8,4,128,512]{2,0,3,1:T(8,128)(2,1)} copy(bf16[8,4,128,512]{3,2,1,0:T(8,128)(2,1)} %bitcast.32) | data formatting | bytes 8388608 | tf_op jit(solution)/shard_map/reshape | solution.py:408
  335.9 6.7 %multiply_reduce_fusion = (f32[1024]{0:T(1024)S(1)}, f32[1024,2048]{1,0:T(8,128)S(1)}) fusion(bf16[256,8,8,128]{3,2,1,0:T(8,128)(2,1)} %bitcast.33, s32[1024]{0:T(1024)S(1)} %fusion.36), kind=kOutput, calls=%fused_computation.3 | convolution fusion | flops 4300209152 | bytes 12591104 | tf_op jit(solution)/shard_map/dot_general | solution.py:417
  342.7 0.0 copy-start.13
  342.7 10.7 %add_convert_fusion.1 = bf16[1024,2048]{1,0:T(8,128)(2,1)} fusion(f32[1024,2048]{1,0:T(8,128)S(1)} %bitcast.31, f32[1024,2048]{1,0:T(8,128)} %reshape.134, f32[1024,2048]{1,0:T(8,128)S(1)} %get-tuple-element.25, f32[2048]{0:T(1024)S(1)} %copy-done.15, f32[1024]{0:T(1024)S(1)} %add_rsqrt_fusion), kind=kLoop, calls=%fused_computation.2 | loop fusion | flops 10485760 | bytes 29372416 | tf_op jit(solution)/shard_map/convert_element_type | solution.py:438
  353.3 0.0 copy-done.13
  353.4 3.6 fusion.59
  357.0 0.1 copy-done.10
  357.1 1.3 fusion.58
  358.4 0.8 fusion.5
  359.2 0.0 copy-start.17
  359.2 0.0 copy-start.18
  359.2 0.7 fusion.11
  359.9 0.6 copy-done.6
  360.4 0.5 fusion.60
  360.9 0.9 fusion.61.x
  361.8 9.6 %shard_map.151 = f32[8,128]{1,0:T(8,128)} custom-call(f32[8,128]{1,0:T(8,128)} %fusion.61.x), custom_call_target="tpu_custom_call" | custom-call | tf_op jit(solution)/shard_map/pallas_call | solution.py:152
  371.5 1.1 fusion.57
  372.6 0.2 fusion.47
  372.8 0.6 fusion.43
  373.3 0.1 mul.189
  373.4 0.8 mul.190
  374.2 1.1 multiply_reduce_fusion.2
  375.3 5.4 %mul.196 = f32[32,8,4,2048]{3,2,1,0:T(4,128)} broadcast(f32[8,2048]{1,0:T(8,128)S(1)} %fusion.43), dimensions={1,3} | broadcast | bytes 8454144 | tf_op jit(solution)/shard_map/mul | solution.py:468
  380.7 10.0 %mul.197 = f32[1024,2048]{1,0:T(8,128)} reshape(f32[32,8,4,2048]{3,2,1,0:T(4,128)} %mul.196) | data formatting | bytes 16777216 | tf_op jit(solution)/shard_map/mul | solution.py:468
  390.7 4.8 %fusion = f32[1024,256]{1,0:T(8,128)S(1)} fusion(bf16[256,2048]{1,0:T(8,128)(2,1)S(1)} %copy-done.6, f32[1024,2048]{1,0:T(8,128)} %mul.197, f32[1024]{0:T(1024)S(1)} %div.99), kind=kOutput, calls=%fused_computation.4 | convolution fusion | flops 1077936128 | bytes 10489856 | tf_op jit(solution)/shard_map/dot_general | solution.py:471
  395.5 0.0 copy-start.14
  395.5 1.5 fusion.12
  397.0 0.0 copy-start.1
  397.1 1.4 add_convert_fusion
  398.4 0.0 copy-start.12
  398.4 38.8 %shard_map.152 = f32[32,2048]{1,0:T(8,128)S(1)} custom-call(bf16[32,32,2048]{2,1,0:T(8,128)(2,1)S(1)} %bitcast.29), custom_call_target="tpu_custom_call" | custom-call | tf_op jit(solution)/shard_map/pallas_call | solution.py:266
  437.2 1.2 multiply_reduce_fusion.1
  438.4 1.1 add_multiply_fusion
  439.5 0.8 reshape.138
  (43 shorter events, 0.2 us)
Async XLA Ops:
  7.2 223.2 %copy-start = (bf16[256,4096]{1,0:T(8,128)(2,1)S(1)}, bf16[256,4096]{1,0:T(8,128)(2,1)}, u32[]{:S(2)}) copy-start(bf16[256,4096]{1,0:T(8,128)(2,1)} %param.21) | copy-start | bytes 6291460
  7.2 133.8 %copy-start.16 = (s32[8]{0:T(128)S(1)}, s32[8]{0:T(128)}, u32[]{:S(2)}) copy-start(s32[8]{0:T(128)} %param.18) | copy-start | bytes 100
  7.2 321.1 %all-gather.3.cloned.1.call-start = ((), (), s32[]{:S(2)}) async-start(), calls=%async_computation | async-start | bytes 4325376 | tf_op jit(solution)/shard_map/all_gather | solution.py:406
  142.5 1.6 copy-start.2
  144.1 1.6 copy-start.3
  225.3 5.0 %copy-start.19 = (s32[8]{0:T(128)S(1)}, s32[8]{0:T(128)}, u32[]{:S(2)}) copy-start(s32[8]{0:T(128)} %param.19) | copy-start | bytes 100
  335.9 6.8 %slice-start = ((s8[8388608]{0:T(1024)(128)(4,1)}), s8[4194304]{0:T(1024)(128)(4,1)S(1)}, s32[]{:S(2)}) async-start(s8[8388608]{0:T(1024)(128)(4,1)} %bitcast.30), calls=%async_computation.1 | async-start | bytes 8388608
  335.9 6.8 %slice-start.1 = ((s8[8388608]{0:T(1024)(128)(4,1)}), s8[4194304]{0:T(1024)(128)(4,1)S(1)}, s32[]{:S(2)}) async-start(s8[8388608]{0:T(1024)(128)(4,1)} %bitcast.30), calls=%async_computation.2 | async-start | bytes 8388608
  335.9 6.8 %copy-start.15 = (f32[2048]{0:T(1024)S(1)}, f32[2048]{0:T(1024)}, u32[]{:S(2)}) copy-start(f32[2048]{0:T(1024)} %param.22) | copy-start | bytes 24580
  342.6 15.8 %copy-start.4 = (f32[1024,2048]{1,0:T(8,128)}, f32[1024,2048]{1,0:T(8,128)S(1)}, u32[]{:S(2)}) copy-start(f32[1024,2048]{1,0:T(8,128)S(1)} %get-tuple-element.25) | copy-start | bytes 25165828
  342.7 10.7 %copy-start.13 = (bf16[2048,256]{1,0:T(8,128)(2,1)S(1)}, bf16[2048,256]{1,0:T(8,128)(2,1)}, u32[]{:S(2)}) copy-start(bf16[2048,256]{1,0:T(8,128)(2,1)} %param.24) | copy-start | bytes 3145732
  353.4 3.6 copy-start.7
  353.4 3.7 copy-start.10
  357.1 2.1 copy-start.8
  359.2 1.2 copy-start.6
  359.2 1.7 copy-start.5
  359.2 12.3 %copy-start.17 = (f32[128]{0:T(128)S(1)}, f32[128]{0:T(128)}, u32[]{:S(2)}) copy-start(f32[128]{0:T(128)} %param.27) | copy-start | bytes 1540
  359.2 13.6 %copy-start.18 = (s32[8]{0:T(128)S(1)}, s32[8]{0:T(128)}, u32[]{:S(2)}) copy-start(s32[8]{0:T(128)} %param.20) | copy-start | bytes 100
  390.7 4.8 %copy-start.9 = (f32[1024,256]{1,0:T(8,128)S(1)}, f32[1024,256]{1,0:T(8,128)}, u32[]{:S(2)}) copy-start(f32[1024,256]{1,0:T(8,128)} %copy-done.8) | copy-start | bytes 3145732
  390.7 4.8 %copy-start.11 = (bf16[2048,256]{1,0:T(8,128)(2,1)S(1)}, bf16[2048,256]{1,0:T(8,128)(2,1)}, u32[]{:S(2)}) copy-start(bf16[2048,256]{1,0:T(8,128)(2,1)} %param.23) | copy-start | bytes 3145732
  395.5 1.5 copy-start.14
  397.0 43.3 %copy-start.1 = (bf16[256,4096]{1,0:T(8,128)(2,1)S(1)}, bf16[256,4096]{1,0:T(8,128)(2,1)}, u32[]{:S(2)}) copy-start(bf16[256,4096]{1,0:T(8,128)(2,1)} %param.21) | copy-start | bytes 6291460
  398.4 40.0 %copy-start.12 = (f32[32,2048]{1,0:T(8,128)S(1)}, f32[32,2048]{1,0:T(8,128)}, u32[]{:S(2)}) copy-start(f32[32,2048]{1,0:T(8,128)} %mul.190) | copy-start | bytes 786436
Sparse Core Ops, SparseCore 0:
  225.5 102.7 all-gather.2

commit v2 on v1

--- a/solution.py
+++ b/solution.py
@@ -281,6 +281,79 @@
     )(x)
 
 
+def collect_kernel(n, orders, x, out, own_sem, send_sem, recv_sem):
+    me = lax.axis_index("head")
+    bits = n.bit_length() - 1
+    height = x.shape[0] // len(orders)
+    bit_of = [(me // (1 << b)) % 2 for b in range(bits)]
+
+    def flipped(r):
+        result = me
+        for b in range(bits):
+            if (r >> b) & 1:
+                result = result + (1 << b) * (1 - 2 * bit_of[b])
+        return result
+
+    barrier = pltpu.get_barrier_semaphore()
+    for b in range(bits):
+        pl.semaphore_signal(
+            barrier, inc=1, device_id={"head": flipped(1 << b)}, device_id_type=MESH
+        )
+    pl.semaphore_wait(barrier, bits)
+
+    own = pltpu.make_async_copy(x, out.at[me], own_sem)
+    own.start()
+    everything = []
+
+    def copy_of(stream, r, bit):
+        rows = pl.ds(stream * height, height)
+        return pltpu.make_async_remote_copy(
+            src_ref=x.at[rows] if r == 0 else out.at[flipped(r), rows],
+            dst_ref=out.at[flipped(r), rows],
+            send_sem=send_sem.at[stream, r | (1 << bit)],
+            recv_sem=recv_sem.at[stream, r | (1 << bit)],
+            device_id={"head": flipped(1 << bit)},
+            device_id_type=MESH,
+        )
+
+    def pass_on(stream, r, later):
+        for bit in later:
+            copy = copy_of(stream, r, bit)
+            copy.start()
+            everything.append(copy)
+
+    for stream, order in enumerate(orders):
+        pass_on(stream, 0, order)
+    held = [[0] for _ in orders]
+    for stage in range(bits):
+        for i in range(1 << stage):
+            for stream, order in enumerate(orders):
+                bit = order[stage]
+                r = held[stream][i]
+                copy_of(stream, r, bit).wait_recv()
+                pass_on(stream, r | (1 << bit), order[stage + 1 :])
+        for stream, order in enumerate(orders):
+            held[stream] += [r | (1 << order[stage]) for r in held[stream]]
+    for copy in everything:
+        copy.wait_send()
+    own.wait()
+
+
+def collect_over(n, x, orders):
+    return pl.pallas_call(
+        functools.partial(collect_kernel, n, orders),
+        out_shape=jax.ShapeDtypeStruct((n,) + x.shape, x.dtype),
+        in_specs=[pl.BlockSpec(memory_space=pl.ANY)],
+        out_specs=pl.BlockSpec(memory_space=pl.ANY),
+        scratch_shapes=[
+            pltpu.SemaphoreType.DMA,
+            pltpu.SemaphoreType.DMA((len(orders), n)),
+            pltpu.SemaphoreType.DMA((len(orders), n)),
+        ],
+        compiler_params=pltpu.CompilerParams(collective_id=4, has_side_effects=True),
+    )(x)
+
+
 def attend_kernel(head_dim, q_ref, k_ref, v_ref, valid_ref, att_ref, pooled_ref, key_scratch):
     tile = pl.program_id(1)
     lanes = q_ref.shape[1]
@@ -317,10 +390,12 @@
         result = jnp.dot(weights, v_ref[...], preferred_element_type=jnp.float32)
         result = result * valid
         mixed.append(result)
-        att_ref[h] = result[:, h * head_dim : (h + 1) * head_dim].astype(jnp.bfloat16)
     joined = mixed[0]
     for h in range(1, heads):
         joined = jnp.where(lane >= h * head_dim, mixed[h], joined)
+    turned = joined.T.astype(jnp.bfloat16)
+    for h in range(heads):
+        att_ref[h] = turned[h * head_dim : (h + 1) * head_dim, :]
     windows = qtile // POOL
     row = lax.broadcasted_iota(jnp.int32, (windows, qtile), 0)
     slot = lax.broadcasted_iota(jnp.int32, (windows, qtile), 1)
@@ -339,7 +414,7 @@
         functools.partial(attend_kernel, head_dim),
         grid=(cols // lanes, length // qtile),
         out_shape=(
-            jax.ShapeDtypeStruct((heads, length, head_dim), jnp.bfloat16),
+            jax.ShapeDtypeStruct((heads, head_dim, length), jnp.bfloat16),
             jax.ShapeDtypeStruct((length // POOL, cols), jnp.bfloat16),
         ),
         in_specs=[
@@ -349,7 +424,7 @@
             pl.BlockSpec((length, lanes), lambda p, t: (0, 0)),
         ],
         out_specs=[
-            pl.BlockSpec((2, qtile, head_dim), lambda p, t: (p, t, 0)),
+            pl.BlockSpec((2, head_dim, qtile), lambda p, t: (p, 0, t)),
             pl.BlockSpec((qtile // POOL, lanes), lambda p, t: (t, p)),
         ],
         scratch_shapes=[pltpu.VMEM((2, length, lanes), jnp.bfloat16)],
@@ -403,7 +478,9 @@
         head_dim,
     )
     row_count = jnp.sum(valid_all.reshape(devices, showers, per_device, POOL), axis=3)
-    pooled_all = lax.all_gather(pooled, "head", axis=0, tiled=False)
+    bits = devices.bit_length() - 1
+    high = list(range(bits - 1, 2, -1))
+    pooled_all = collect_over(devices, pooled, (high[::-1] + [2, 1, 0], high[::-1] + [1, 2, 0]))
     by_shower = (
         pooled_all.reshape(showers, groups, windows, cols)
         .transpose(0, 2, 1, 3)
@@ -427,9 +504,9 @@
     inverse_rms = lax.rsqrt(jnp.mean(pooled_rows * pooled_rows, axis=1, keepdims=True) + epsilon)
 
     def by_row(table):
-        wide = jnp.broadcast_to(
-            table[None, :, None, :], (devices, showers, per_device, table.shape[1])
-        )
+        rows = jnp.broadcast_to(table[:, None, :], (showers, per_device, table.shape[1]))
+        rows = lax.optimization_barrier(rows.reshape(1, showers * per_device, table.shape[1]))
+        wide = jnp.broadcast_to(rows, (devices,) + rows.shape[1:])
         return wide.reshape(row_total, table.shape[1])
 
     unit_rows = pooled_rows * inverse_rms
@@ -465,9 +542,7 @@
     probability = exponent / jnp.sum(exponent, axis=1, keepdims=True)
     feature_grad = jnp.dot(target - probability, class_matrix.T, precision=HIGHEST)
     row_share = row_count / shower_counts[None, :, None]
-    row_grads = (row_share[:, :, :, None] * feature_grad[None, :, None, :]).reshape(
-        row_total, model_width
-    )
+    row_grads = row_share.reshape(row_total, 1) * by_row(feature_grad)
     hidden_grad = jnp.dot(
         row_grads.astype(jnp.bfloat16), down_weight.T, preferred_element_type=jnp.float32
     )
@@ -480,8 +555,6 @@
         jnp.dot(gate_grad, gate_weight.T, preferred_element_type=jnp.float32)
         + jnp.dot(up_grad, up_weight.T, preferred_element_type=jnp.float32)
     ).astype(jnp.bfloat16)
-    bits = devices.bit_length() - 1
-    high = list(range(bits - 1, 2, -1))
     rows_here = showers * per_device
     normed_grad = reduce_over(
         devices,
@@ -508,7 +581,7 @@
         unit_grad - own_units * jnp.mean(unit_grad * own_units, axis=1, keepdims=True)
     )
     guidance = windows * (own_row_grads + pooled_grad)
-    return (attention, guidance.reshape(showers, per_device, model_width))
+    return (attention.transpose(0, 2, 1), guidance.reshape(showers, per_device, model_width))
 
 
 def solution(mesh):

time: 448 us -> 383 us (0.85)
  Pallas kernels: 260 us -> 329 us
  waiting for transfers between devices: 65.8 us -> 0 us
  local copies, waits for them, and re-layouts: 66.7 us -> 23.4 us
  between operations: 14.4 us -> 1.04 us
  other arithmetic: 15.6 us -> 9.12 us
  matrix products: 24.2 us -> 19.6 us
    pallas_call x0 -> x1, Pallas kernels: none -> 68.1 us  [collect_over(): pl.pallas_call(functools.partial(collect_kernel, n, orders), out_shape=ja...]
    all_gather x1 -> x0, waiting for transfers between devices: 65.8 us -> none  [body(): pooled_all = lax.all_gather(pooled, 'head', axis=0, tiled=False)]
    reshape x3 -> x4, local copies, waits for them, and re-layouts: 20.8 us -> 2.71 us  [the longest x3 1.93 us: by_row(): rows.reshape(1, showers * per_device, table.shape[1])]
    mul x2 -> x0, local copies, waits for them, and re-layouts: 15.4 us -> none  [body(): row_share[:, :, :, None] * feature_grad[None, :, None, :]]
    broadcast_in_dim x3 -> x2, local copies, waits for them, and re-layouts: 10.7 us -> 0.09 us  [by_row(): jnp.broadcast_to(table[:, None, :], (showers, per_device, table.shape[1]))]
    convert_element_type x1, other arithmetic: 10.7 us -> 2.12 us  [body(): normed = (unit_rows * norm_gain * by_row(scales) + by_row(modulation[:, :...]
  transfers between devices with their start and end apart: 1 -> 0, of which waited for: 1 -> 0; matrix products, arithmetic and copies ran while one was open for 8% -> 0% of each run, Pallas kernels for 0% -> 0%
where the time goes in v2:
time: 383 us; the launch traced here: 382 us
  Pallas kernels  329 us (86%)
  local copies, waits for them, and re-layouts  23.4 us (6%)
  matrix products  19.6 us (5%)
  other arithmetic  9.12 us (2%)
    pallas_call x1, Pallas kernels, swap(): pl.pallas_call(functools.partial(swap_kernel, n), out_shape=(field, field...  133 us
    pallas_call x1, Pallas kernels, attend(): pl.pallas_call(functools.partial(attend_kernel, head_dim), grid=(cols //...  79.7 us
    pallas_call x1, Pallas kernels, collect_over(): pl.pallas_call(functools.partial(collect_kernel, n, orders), out_shape=ja...  68.1 us
    pallas_call x1, Pallas kernels, reduce_over(): pl.pallas_call(functools.partial(reduce_kernel_entry, n, plan), out_shape...  38.7 us
    pallas_call x1, Pallas kernels, total_over(): pl.pallas_call(functools.partial(total_kernel, n), out_shape=jax.ShapeDty...  9.84 us
    unnamed x38, local copies, waits for them, and re-layouts  7.95 us

profile of v2, /device:TPU:0, one launch (start us, length us, event | category | flops | bytes accessed | tf_op | source)
XLA Modules:
  0.0 382.0 jit_solution(508057454627685155)
XLA Ops:
  0.6 0.0 copy-start
  0.7 0.8 convert_element_type.42
  1.5 0.7 convert_element_type.45
  2.1 0.1 fusion.30
  2.3 1.3 pad.4.f
  3.6 0.0 copy-done
  3.6 0.4 fusion.39
  4.0 0.1 div.82.clone
  4.0 0.1 div.98
  4.2 0.0 copy-start.16
  4.2 0.1 reshape.154
  4.3 0.1 reshape.147
  4.5 0.1 reshape.149
  4.6 132.5 %shard_map.149 = (bf16[2048,512]{1,0:T(8,128)(2,1)}, bf16[2048,512]{1,0:T(8,128)(2,1)}, bf16[2048,512]{1,0:T(8,128)(2,1)}, s32[32,8,128]{2,1,0:T(8,128)}) custom-call(bf16[8,64,2048]{2,1,0:T(8,128)(2,1)} %q.1, bf16[8,64,2048]{2,1,0:T(8,128)(2,1)} %k.1, bf16[8,64,2048]{2,1,0:T(8,128)(2,1)} %v.1, s32[8,128]{1,0:T(8,128)} %pad.4.f), custom_call_target="tpu_custom_call" | custom-call | tf_op jit(solution)/shard_map/pallas_call | solution.py:106
  137.1 0.0 copy-done.16
  137.1 1.0 fusion.22
  138.1 0.1 dynamic-slice_reduce_fusion
  138.2 0.1 broadcast_in_dim.20
  138.2 0.1 copy.18
  138.4 0.1 bitcast_reduce_fusion
  138.5 0.2 fusion.23
  138.6 0.1 mul.162
  138.7 0.1 copy.19
  138.9 0.1 mul.164
  139.0 0.3 broadcast_in_dim.21.valid_ref
  139.3 0.0 copy-start.1
  139.3 1.6 copy-done.1
  140.9 1.6 copy-done.2
  142.5 79.7 %shard_map.150 = (bf16[8,64,2048]{2,1,0:T(8,128)(2,1)}, bf16[128,512]{1,0:T(8,128)(2,1)S(1)}) custom-call(bf16[2048,512]{1,0:T(8,128)(2,1)S(1)} %copy-done.1, bf16[2048,512]{1,0:T(8,128)(2,1)S(1)} %copy-done.2, bf16[2048,512]{1,0:T(8,128)(2,1)} %get-tuple-element.10.v_ref, f32[2048,128]{1,0:T(8,128)S(1)} %broadcast_in_dim.21.valid_ref), custom_call_target="tpu_custom_call" | custom-call | tf_op jit(solution)/shard_map/pallas_call | solution.py:413
  222.2 0.7 copy-done.3
  222.9 68.1 %shard_map.151 = bf16[32,128,512]{2,1,0:T(8,128)(2,1)} custom-call(bf16[128,512]{1,0:T(8,128)(2,1)} %copy-done.3), custom_call_target="tpu_custom_call" | custom-call | tf_op jit(solution)/shard_map/pallas_call | solution.py:343
  290.9 7.6 %copy.20 = bf16[8,4,128,512]{2,0,3,1:T(8,128)(2,1)} copy(bf16[8,4,128,512]{3,2,1,0:T(8,128)(2,1)} %bitcast.47) | data formatting | bytes 8388608 | tf_op jit(solution)/shard_map/reshape | solution.py:485
  298.5 6.6 %multiply_reduce_fusion = (f32[1024]{0:T(1024)S(1)}, f32[1024,2048]{1,0:T(8,128)S(1)}) fusion(bf16[256,8,8,128]{3,2,1,0:T(8,128)(2,1)} %bitcast.48, s32[1024]{0:T(1024)S(1)} %fusion.36), kind=kOutput, calls=%fused_computation.6 | convolution fusion | flops 4300209152 | bytes 12591104 | tf_op jit(solution)/shard_map/dot_general | solution.py:494
  305.1 0.0 copy-start.4
  305.2 0.1 multiply_reduce_fusion.2
  305.3 0.8 fusion.5
  306.1 2.2 copy-done.4
  308.4 2.1 fusion.1
  310.5 0.0 copy-start.13
  310.5 1.3 fusion.58
  311.8 1.3 fusion.59
  313.1 1.0 copy-done.6
  314.1 0.7 fusion.11
  314.8 0.6 copy-done.11
  315.3 0.5 fusion.60
  315.8 0.9 fusion.61.x
  316.8 9.8 %shard_map.152 = f32[8,128]{1,0:T(8,128)} custom-call(f32[8,128]{1,0:T(8,128)} %fusion.61.x), custom_call_target="tpu_custom_call" | custom-call | tf_op jit(solution)/shard_map/pallas_call | solution.py:152
  326.6 0.0 copy-done.17
  326.6 1.5 fusion.57
  328.1 0.2 fusion.47
  328.3 1.6 fusion.43
  329.9 0.8 mul.181
  330.7 1.7 reshape.151
  332.4 1.7 mul.182
  334.2 1.6 fusion
  335.8 0.0 copy-start.9
  335.8 1.3 fusion.62
  337.1 0.2 copy-done.9
  337.3 1.5 fusion.12
  338.8 1.4 add_convert_fusion
  340.2 38.7 %shard_map.153 = f32[32,2048]{1,0:T(8,128)S(1)} custom-call(bf16[32,32,2048]{2,1,0:T(8,128)(2,1)S(1)} %bitcast.46), custom_call_target="tpu_custom_call" | custom-call | tf_op jit(solution)/shard_map/pallas_call | solution.py:266
  379.0 1.2 multiply_reduce_fusion.1
  380.1 1.1 add_multiply_fusion
  381.2 0.8 reshape.155
  (32 shorter events, 0.2 us)
Async XLA Ops:
  0.6 2.9 copy-start
  4.2 133.0 %copy-start.16 = (s32[8]{0:T(128)S(1)}, s32[8]{0:T(128)}, u32[]{:S(2)}) copy-start(s32[8]{0:T(128)} %param.18) | copy-start | bytes 100
  139.3 1.6 copy-start.1
  140.9 1.6 copy-start.2
  222.2 0.7 copy-start.3
  305.1 3.2 copy-start.4
  305.3 3.0 copy-start.15
  308.4 2.1 copy-start.8
  310.5 1.3 copy-start.13
  313.1 1.0 copy-start.6
  314.1 1.2 copy-start.11
  314.1 1.7 copy-start.5
  314.1 12.5 %copy-start.17 = (f32[128]{0:T(128)S(1)}, f32[128]{0:T(128)}, u32[]{:S(2)}) copy-start(f32[128]{0:T(128)} %param.27) | copy-start | bytes 1540
  314.1 14.2 %copy-start.18 = (s32[8]{0:T(128)S(1)}, s32[8]{0:T(128)}, u32[]{:S(2)}) copy-start(s32[8]{0:T(128)} %param.20) | copy-start | bytes 100
  334.2 1.6 copy-start.12
  335.8 1.3 copy-start.7
  335.8 1.5 copy-start.9
  337.3 1.5 copy-start.14
  340.2 39.9 %copy-start.10 = (f32[32,2048]{1,0:T(8,128)S(1)}, f32[32,2048]{1,0:T(8,128)}, u32[]{:S(2)}) copy-start(f32[32,2048]{1,0:T(8,128)} %mul.182) | copy-start | bytes 786436
